TPU v7x, 32 devices: a whole 2x2x4 slice. The times are simulated.
32 devices in a mesh: sub: 4 (over z), row: 2 (over core), col: 4 (over y, x).
Axes of the slice: x: 2, y: 2, z: 4, core: 2. Of those that a mesh axis runs over, the one named last changes fastest.
Arguments:
- factor_cols: bfloat16 [4, 2, 2048, 4096], P('sub', None, 'col', 'row'), may hold values from -0.09375 to 0.09375
- block_pattern: int32 [4, 16, 16], P('sub'), may hold values 0 or 1
- diag_inverse: float32 [4, 4096, 2048], P('sub', ('row', 'col')), may hold values from -1 to 2
- coupling_cols: bfloat16 [4, 2, 2048, 1024], P('sub', 'row', 'col'), may hold values from -0.09375 to 0.09375
- separator_rows: int32 [4, 1024], P('sub'), may hold values from 0 to 1535, as said below
- root_inverse: float32 [1536, 1536], P('col'), may hold values from -1 to 2
- right_side: float32 [4, 4096, 128], P('sub', 'row'), may hold values from -6 to 6
- root_right: float32 [1536, 128], P('col'), may hold values from -6 to 6
Outputs:
- solution: float32 [4, 4096, 128], P('sub', ('row', 'col'))
- root_solution: float32 [1536, 128], P('col')
Inputs may be any that keep to these rules, and one draw needn't show every extreme that they name: `separator_rows`: within one section the 1024 entries are distinct.
All inputs are finite; a program needn't handle non-finite values. No bound on the sum of `block_pattern` on one device may be relied on, other than what follows from the above.
Results may differ from a plain program's by a relative error of at most 0.003.
Values may be sent and summed in bfloat16 or wider, within the bound.
A program may use at most 64 MiB of HBM per device.

v0:
```python
import jax
import jax.numpy as jnp
from jax import lax
from jax.sharding import PartitionSpec as P

BLOCK = 256
SEPARATOR = 1536
precise = lax.Precision.HIGHEST
first_axes = (((0,), (0,)), ((), ()))


def spread(block, axis, source):
    block = jnp.where(lax.axis_index(axis) == source, block, jnp.zeros_like(block))
    return lax.psum(block, axis)


def shards(
    factor_cols,
    block_pattern,
    diag_inverse,
    coupling_cols,
    separator_rows,
    root_inverse,
    right_side,
    root_right,
):
    factor = factor_cols[0]
    table = block_pattern[0]
    inverse = diag_inverse[0]
    couple_own = coupling_cols[0, 0]
    right_rows = right_side[0]
    rows_sep = separator_rows[0]
    panel_count, col_width, panel_rows = factor.shape
    sources = right_rows.shape[1]
    block_count = table.shape[1]
    row_id = lax.axis_index("row")
    col_id = lax.axis_index("col")
    sub_id = lax.axis_index("sub")
    own_blocks = lax.dynamic_slice_in_dim(
        table, row_id * (panel_rows // BLOCK), panel_rows // BLOCK, 0
    ).astype(jnp.float32)
    row_mask = jnp.repeat(own_blocks, BLOCK, axis=0)
    col_pos = (
        jnp.arange(panel_count)[:, None] * panel_rows
        + col_id * col_width
        + jnp.arange(col_width)[None, :]
    )
    selector = (jnp.arange(block_count)[:, None, None] == (col_pos // BLOCK)[None]).astype(
        jnp.float32
    )
    pattern_mask = jnp.einsum("in,nqj->qji", row_mask, selector)
    below_mask = (jnp.arange(panel_count) < row_id).astype(jnp.float32)[:, None, None]
    masked = factor * (pattern_mask * below_mask).astype(jnp.bfloat16)
    zero_panel = jnp.zeros((panel_rows, sources), jnp.float32)
    zero_share = jnp.zeros((col_width, sources), jnp.float32)

    def forward(current, carried):
        accumulated, solved = carried
        panel_total = lax.psum(accumulated, "col")
        solved = lax.cond(
            row_id == current,
            lambda values: jnp.dot(
                inverse, right_rows - values, precision=precise, preferred_element_type=jnp.float32
            ),
            lambda values: solved,
            panel_total,
        )
        received = spread(solved.astype(jnp.bfloat16), "row", current)
        factor_now = lax.dynamic_index_in_dim(masked, current, 0, keepdims=False)
        accumulated = accumulated + lax.dot_general(
            factor_now, received, first_axes, preferred_element_type=jnp.float32
        )
        return (accumulated, solved)

    accumulated, solved = lax.fori_loop(0, panel_count, forward, (zero_panel, zero_share))
    own_low = solved.astype(jnp.bfloat16)
    sep_partial = lax.dot_general(
        couple_own, own_low, first_axes, preferred_element_type=jnp.float32
    )
    onehot = (jnp.arange(SEPARATOR)[:, None] == rows_sep[None, :]).astype(jnp.float32)
    mapped = jnp.dot(onehot, sep_partial, precision=precise, preferred_element_type=jnp.float32)
    share_rows = root_inverse.shape[0]
    slice_start = col_id * share_rows
    first_device = ((sub_id == 0) & (row_id == 0)).astype(jnp.float32)
    own_rows = (
        lax.dynamic_slice_in_dim(-mapped, slice_start, share_rows, 0) + first_device * root_right
    )
    root_term = lax.dynamic_update_slice_in_dim(-mapped, own_rows, slice_start, 0)
    root_share = lax.psum_scatter(root_term, "col", scatter_dimension=0, tiled=True)
    root_share = lax.psum(root_share, ("sub", "row"))
    root_rhs = lax.all_gather(root_share, "col", axis=0, tiled=True)
    root_half = jnp.dot(
        root_inverse, root_rhs, precision=precise, preferred_element_type=jnp.float32
    )
    root_part = lax.psum_scatter(
        lax.dot_general(
            root_inverse,
            root_half,
            first_axes,
            precision=precise,
            preferred_element_type=jnp.float32,
        ),
        "col",
        scatter_dimension=0,
        tiled=True,
    )
    root_full = lax.all_gather(root_part.astype(jnp.bfloat16), "col", axis=0, tiled=True).astype(
        root_part.dtype
    )
    picked = lax.dot_general(
        onehot, root_full, first_axes, precision=precise, preferred_element_type=jnp.float32
    ).astype(jnp.bfloat16)
    couple_back = jnp.dot(couple_own, picked, preferred_element_type=jnp.float32)

    def backward(counter, carried):
        finished, panel_low = carried
        current = panel_count - 1 - counter
        factor_now = lax.dynamic_index_in_dim(masked, current, 0, keepdims=False)
        contribution = jnp.dot(factor_now, panel_low, preferred_element_type=jnp.float32)
        own_couple = couple_back * (row_id == current).astype(jnp.float32)
        summed = lax.psum(contribution + own_couple, "row")
        partial_value = lax.cond(
            row_id == current,
            lambda values: lax.dot_general(
                inverse,
                solved - values,
                first_axes,
                precision=precise,
                preferred_element_type=jnp.float32,
            ),
            lambda values: zero_panel,
            summed,
        )
        value = lax.psum_scatter(partial_value, "col", scatter_dimension=0, tiled=True)
        whole_low = lax.all_gather(value.astype(jnp.bfloat16), "col", axis=0, tiled=True)
        active = row_id == current
        finished = jnp.where(active, value, finished)
        panel_low = jnp.where(active, whole_low, panel_low)
        return (finished, panel_low)

    finished, panel_low = lax.fori_loop(
        0, panel_count, backward, (zero_share, zero_panel.astype(jnp.bfloat16))
    )
    return (finished[None], root_part)


def solution(mesh):
    return jax.shard_map(
        shards,
        mesh=mesh,
        in_specs=(
            P("sub", None, "col", "row"),
            P("sub", None, None),
            P("sub", ("row", "col"), None),
            P("sub", "row", "col", None),
            P("sub", None),
            P("col", None),
            P("sub", "row", None),
            P("col", None),
        ),
        out_specs=(P("sub", ("row", "col"), None), P("col", None)),
        check_vma=False,
    )
```

profile of v0, /device:TPU:0, one launch (start us, length us, event | category | flops | bytes accessed | tf_op | source)
XLA Modules:
  0.0 492.3 jit_solution(17336748662876805987)
XLA Ops:
  9.2 5.5 %bitcast_multiply_fusion = bf16[2,512,2048]{2,1,0:T(8,128)(2,1)} fusion(bf16[1,2,512,2048]{3,2,1,0:T(8,128)(2,1)} %param.16, f32[2]{0:T(128)S(1)} %compare_convert_fusion, bf16[2048,16,1]{0,1,2:T(8,128)(2,1)S(1)} %reshape.56, s32[2,512]{1,0:T(2,128)S(1)} %and_select_fusion), kind=kOutput, calls=%fused_computation.24 | convolution fusion | flops 73416704 | bytes 8458248 | tf_op jit(solution)/shard_map/in,nqj->qji/dot_general | solution.py:51
  15.4 178.1 %while.37 = (s32[]{:T(128)}, f32[2048,128]{1,0:T(8,128)}, f32[512,128]{0,1:T(8,128)}, bf16[2,512,2048]{2,1,0:T(8,128)(2,1)}, s32[]{:T(128)}, /*index=5*/f32[2048...) while((s32[]{:T(128)}, f32[2048,128]{1,0:T(8,128)}, ...), condition=%wide.region_5.6_spmd.clone, body=%wide.region_0.5_spmd.clone.sunk | while | flops 1880293376 | bytes 24641860 | solution.py:75
  16.6 58.0 %all-reduce.7.cloned.1.call-done = f32[2048,128]{1,0:T(8,128)} async-done(((f32[2048,128]{1,0:T(8,128)}), f32[2048,128]{1,0:T(8,128)}) %all-reduce.7.cloned.1.call-update) | async-done | bytes 1048592 | tf_op jit(solution)/shard_map/while/body/eval_jaxpr/psum | solution.py:59
  74.5 8.0 %conditional.7 = (f32[512,128]{0,1:T(8,128)}) conditional(s32[]{:T(128)} %convert_element_type.111, f32[512,128]{0,1:T(8,128)} %get-tuple-element.579, (f32[2048,128]{1,0:T(8,128)}, f32[2048,128]{1,0:T(8,128)}, f32[512,2048]{1,0:T(8,128)}) %tuple.109), branch_computations={%region_2.2_spmd.clone, %region_3.3_spmd.clone} | conditional | flops 1610874880 | bytes 6553608
  74.5 8.0 %convolution_bitcast_fusion.1 = f32[512,128]{0,1:T(8,128)} fusion(f32[512,2048]{1,0:T(8,128)} %get-tuple-element.370, f32[2048,128]{1,0:T(8,128)} %get-tuple-element.368, f32[2048,128]{1,0:T(8,128)} %get-tuple-element.369), kind=kOutput, calls=%fused_computation.2 | convolution fusion | flops 1610874880 | bytes 6553600 | tf_op jit(solution)/shard_map/while/body/eval_jaxpr/cond/branch_1_fun/dot_general | solution.py:62
  84.2 18.1 %all-reduce.9.cloned.1.call-done = bf16[512,128]{0,1:T(8,128)(2,1)} async-done(((bf16[512,128]{0,1:T(8,128)(2,1)}), bf16[512,128]{0,1:T(8,128)(2,1)}) %all-reduce.9.cloned.1.call-update) | async-done | bytes 131088 | tf_op jit(solution)/shard_map/while/body/eval_jaxpr/psum | solution.py:14
  102.3 3.3 convolution_add_fusion.2
  108.0 55.2 %all-reduce.7.cloned.1.call-done = f32[2048,128]{1,0:T(8,128)} async-done(((f32[2048,128]{1,0:T(8,128)}), f32[2048,128]{1,0:T(8,128)}) %all-reduce.7.cloned.1.call-update) | async-done | bytes 1048592 | tf_op jit(solution)/shard_map/while/body/eval_jaxpr/psum | solution.py:59
  164.8 25.4 %all-reduce.9.cloned.1.call-done = bf16[512,128]{0,1:T(8,128)(2,1)} async-done(((bf16[512,128]{0,1:T(8,128)(2,1)}), bf16[512,128]{0,1:T(8,128)(2,1)}) %all-reduce.9.cloned.1.call-update) | async-done | bytes 131088 | tf_op jit(solution)/shard_map/while/body/eval_jaxpr/psum | solution.py:14
  190.2 3.3 convolution_add_fusion.2
  199.2 27.3 %reduce-scatter.4.cloned.1.call-done = f32[384,128]{1,0:T(8,128)} async-done(((f32[1536,128]{1,0:T(8,128)}), f32[384,128]{1,0:T(8,128)}) %reduce-scatter.4.cloned.1.call-update) | async-done | bytes 196624 | tf_op jit(solution)/shard_map/reduce_scatter | solution.py:89
  226.6 57.1 %all-reduce.5.cloned.1.call-done = f32[384,128]{1,0:T(8,128)} async-done(((f32[384,128]{1,0:T(8,128)}), f32[384,128]{1,0:T(8,128)}) %all-reduce.5.cloned.1.call-update) | async-done | bytes 196624 | tf_op jit(solution)/shard_map/psum | solution.py:90
  283.7 12.6 %all_gather.16 = f32[1536,128]{1,0:T(8,128)S(1)} all-gather(f32[384,128]{1,0:T(8,128)} %all-reduce.5.cloned.1.call-done), channel_id=1, replica_groups=mesh['sub'=4,'row'=2,'col'=4] {'col'}, dimensions={0}, use_global_device_ids=true | all-gather | bytes 983040 | tf_op jit(solution)/shard_map/all_gather | solution.py:91
  302.5 23.4 %reduce-scatter.6.cloned.1.call-done = f32[384,128]{0,1:T(8,128)} async-done(((f32[1536,128]{0,1:T(8,128)}), f32[384,128]{0,1:T(8,128)}) %reduce-scatter.6.cloned.1.call-update) | async-done | bytes 196624 | tf_op jit(solution)/shard_map/reduce_scatter | solution.py:95
  326.9 10.2 %all_gather.17 = bf16[1536,128]{0,1:T(8,128)(2,1)S(1)} all-gather(bf16[384,128]{0,1:T(8,128)(2,1)S(1)} %convert_element_type.87), channel_id=1, replica_groups=mesh['sub'=4,'row'=2,'col'=4] {'col'}, dimensions={0}, use_global_device_ids=true | all-gather | bytes 491520 | tf_op jit(solution)/shard_map/all_gather | solution.py:107
  341.1 140.1 %while.38 = (s32[]{:T(128)}, f32[512,128]{0,1:T(8,128)}, bf16[2048,128]{0,1:T(8,128)(2,1)}, s32[]{:T(128)}, bf16[2,512,2048]{2,1,0:T(8,128)(2,1)}, /*index=5*/f3...) while((s32[]{:T(128)}, f32[512,128]{0,1:T(8,128)}, ...), condition=%wide.region_14.15_spmd.clone, body=%wide.region_9.14_spmd.clone.sunk | while | flops 1880293376 | bytes 21758288 | solution.py:141
  344.2 18.6 %all-reduce.11.cloned.1.call-done = f32[512,128]{1,0:T(8,128)} async-done(((f32[512,128]{1,0:T(8,128)}), f32[512,128]{1,0:T(8,128)}) %all-reduce.11.cloned.1.call-update) | async-done | bytes 262160 | tf_op jit(solution)/shard_map/while/body/eval_jaxpr/psum | solution.py:121
  363.9 33.8 %reduce-scatter.8.cloned.1.call-done = f32[512,128]{0,1:T(8,128)} async-done(((f32[2048,128]{0,1:T(8,128)}), f32[512,128]{0,1:T(8,128)}) %reduce-scatter.8.cloned.1.call-update) | async-done | bytes 262160 | tf_op jit(solution)/shard_map/while/body/eval_jaxpr/reduce_scatter | solution.py:134
  399.4 10.1 %all_gather.20 = bf16[2048,128]{0,1:T(8,128)(2,1)S(1)} all-gather(bf16[512,128]{0,1:T(8,128)(2,1)S(1)} %get-tuple-element.563), channel_id=1, replica_groups=mesh['sub'=4,'row'=2,'col'=4] {'col'}, dimensions={0}, use_global_device_ids=true | all-gather | bytes 655360 | tf_op jit(solution)/shard_map/while/body/eval_jaxpr/all_gather | solution.py:135
  413.6 18.7 %all-reduce.11.cloned.1.call-done = f32[512,128]{1,0:T(8,128)} async-done(((f32[512,128]{1,0:T(8,128)}), f32[512,128]{1,0:T(8,128)}) %all-reduce.11.cloned.1.call-update) | async-done | bytes 262160 | tf_op jit(solution)/shard_map/while/body/eval_jaxpr/psum | solution.py:121
  432.3 4.7 conditional.8
  432.3 4.7 convolution_bitcast_fusion
  438.0 29.3 %reduce-scatter.8.cloned.1.call-done = f32[512,128]{0,1:T(8,128)} async-done(((f32[2048,128]{0,1:T(8,128)}), f32[512,128]{0,1:T(8,128)}) %reduce-scatter.8.cloned.1.call-update) | async-done | bytes 262160 | tf_op jit(solution)/shard_map/while/body/eval_jaxpr/reduce_scatter | solution.py:134
  469.2 10.0 %all_gather.20 = bf16[2048,128]{0,1:T(8,128)(2,1)S(1)} all-gather(bf16[512,128]{0,1:T(8,128)(2,1)S(1)} %get-tuple-element.563), channel_id=1, replica_groups=mesh['sub'=4,'row'=2,'col'=4] {'col'}, dimensions={0}, use_global_device_ids=true | all-gather | bytes 655360 | tf_op jit(solution)/shard_map/while/body/eval_jaxpr/all_gather | solution.py:135
  (78 shorter events, 43.8 us)
Async XLA Ops:
  8.0 288.3 %copy-start = (f32[384,1536]{1,0:T(8,128)S(1)}, f32[384,1536]{1,0:T(8,128)}, u32[]{:S(2)}) copy-start(f32[384,1536]{1,0:T(8,128)} %param.21) | copy-start | bytes 7077892
  15.4 179.8 %copy-start.7 = (s32[1,1024]{1,0:T(1,128)S(1)}, s32[1,1024]{1,0:T(1,128)}, u32[]{:S(2)}) copy-start(s32[1,1024]{1,0:T(1,128)} %param.20) | copy-start | bytes 12292
  15.4 59.1 %all-reduce.7.cloned.1.call-start = ((), (), s32[]{:S(2)}) async-start(), calls=%async_computation.6 | async-start | bytes 2097152 | tf_op jit(solution)/shard_map/while/body/eval_jaxpr/psum | solution.py:59
  16.5 85.8 %copy-start.1 = (f32[2048,128]{1,0:T(8,128)S(1)}, f32[2048,128]{1,0:T(8,128)}, u32[]{:S(2)}) copy-start(f32[2048,128]{1,0:T(8,128)} %broadcast_select_fusion.7) | copy-start | bytes 3145732 | tf_op jit(solution)/shard_map/while
  16.5 85.8 %all-reduce.9.cloned.1.call-start = ((), (), s32[]{:S(2)}) async-start(), calls=%async_computation.7 | async-start | bytes 262144 | tf_op jit(solution)/shard_map/while/body/eval_jaxpr/psum | solution.py:14
  105.6 57.6 %all-reduce.7.cloned.1.call-start = ((), (), s32[]{:S(2)}) async-start(), calls=%async_computation.6 | async-start | bytes 2097152 | tf_op jit(solution)/shard_map/while/body/eval_jaxpr/psum | solution.py:59
  107.9 82.4 %copy-start.1 = (f32[2048,128]{1,0:T(8,128)S(1)}, f32[2048,128]{1,0:T(8,128)}, u32[]{:S(2)}) copy-start(f32[2048,128]{1,0:T(8,128)} %broadcast_select_fusion.7) | copy-start | bytes 3145732 | tf_op jit(solution)/shard_map/while
  107.9 82.3 %all-reduce.9.cloned.1.call-start = ((), (), s32[]{:S(2)}) async-start(), calls=%async_computation.7 | async-start | bytes 262144 | tf_op jit(solution)/shard_map/while/body/eval_jaxpr/psum | solution.py:14
  193.6 4.6 copy-start.6
  193.6 32.9 %reduce-scatter.4.cloned.1.call-start = ((), (), s32[]{:S(2)}) async-start(), calls=%async_computation.3 | async-start | bytes 983040 | tf_op jit(solution)/shard_map/reduce_scatter | solution.py:89
  198.2 0.9 copy-start.5
  199.2 84.6 %all-reduce.5.cloned.1.call-start = ((), (), s32[]{:S(2)}) async-start(), calls=%async_computation.4 | async-start | bytes 393216 | tf_op jit(solution)/shard_map/psum | solution.py:90
  226.5 75.2 %copy-start.3 = (f32[512,128]{0,1:T(8,128)S(1)}, f32[512,128]{0,1:T(8,128)}, u32[]{:S(2)}) copy-start(f32[512,128]{0,1:T(8,128)} %get-tuple-element.430) | copy-start | bytes 786436
  226.5 99.4 %reduce-scatter.6.cloned.1.call-start = ((), (), s32[]{:S(2)}) async-start(), calls=%async_computation.5 | async-start | bytes 983040 | tf_op jit(solution)/shard_map/reduce_scatter | solution.py:95
  302.5 35.6 %copy-start.4 = (bf16[1,1,512,1024]{3,2,1,0:T(8,128)(2,1)S(1)}, bf16[1,1,512,1024]{3,2,1,0:T(8,128)(2,1)}, u32[]{:S(2)}) copy-start(bf16[1,1,512,1024]{3,2,1,0:T(8,128)(2,1)} %param.19) | copy-start | bytes 3145732
  341.1 21.6 %all-reduce.11.cloned.1.call-start = ((), (), s32[]{:S(2)}) async-start(), calls=%async_computation.8 | async-start | bytes 524288 | tf_op jit(solution)/shard_map/while/body/eval_jaxpr/psum | solution.py:121
  344.1 53.5 %reduce-scatter.8.cloned.1.call-start = ((), (), s32[]{:S(2)}) async-start(), calls=%async_computation.9 | async-start | bytes 1310720 | tf_op jit(solution)/shard_map/while/body/eval_jaxpr/reduce_scatter | solution.py:134
  362.9 1.0 copy-start.2
  410.4 21.9 %all-reduce.11.cloned.1.call-start = ((), (), s32[]{:S(2)}) async-start(), calls=%async_computation.8 | async-start | bytes 524288 | tf_op jit(solution)/shard_map/while/body/eval_jaxpr/psum | solution.py:121
  413.6 53.8 %reduce-scatter.8.cloned.1.call-start = ((), (), s32[]{:S(2)}) async-start(), calls=%async_computation.9 | async-start | bytes 1310720 | tf_op jit(solution)/shard_map/while/body/eval_jaxpr/reduce_scatter | solution.py:134
  437.0 1.0 copy-start.2
Sparse Core Ops, SparseCore 0:
  19.3 55.1 all-reduce.6
  84.3 17.9 all-reduce.8
  109.5 53.6 all-reduce.6
  165.9 24.2 all-reduce.8
  344.5 18.2 all-reduce.10
  365.5 32.1 reduce-scatter.7
  414.1 18.1 all-reduce.10
  438.1 29.1 reduce-scatter.7
Sparse Core Ops, SparseCore 1:
  199.2 27.2 reduce-scatter.3
  228.7 55.0 all-reduce.4
  301.8 24.2 reduce-scatter.5
where the time goes:
time: 493 us; the launch traced here: 492 us
  waiting for transfers between devices  365 us (74%)
  matrix products  43.2 us (9%)
  blocking collectives  42.9 us (9%)
  between operations  15.8 us (3%)
  other arithmetic  14.9 us (3%)
  local copies, waits for them, and re-layouts  10 us (2%)
    psum x2, waiting for transfers between devices, forward(): panel_total = lax.psum(accumulated, 'col')  113 us
    reduce_scatter x2, waiting for transfers between devices, backward(): lax.psum_scatter(partial_value, 'col', scatter_dimension=0, tiled=True)  63.1 us
    psum x1, waiting for transfers between devices, shards(): root_share = lax.psum(root_share, ('sub', 'row'))  57.1 us
    psum x2, waiting for transfers between devices, spread(): return lax.psum(block, axis)  43.5 us
    psum x2, waiting for transfers between devices, backward(): summed = lax.psum(contribution + own_couple, 'row')  37.3 us
    reduce_scatter x1, waiting for transfers between devices, shards(): lax.psum_scatter(root_term, 'col', scatter_dimension=0, tiled=True)  27.3 us
    reduce_scatter x1, waiting for transfers between devices, shards(): lax.psum_scatter(lax.dot_general(root_inverse, root_half, first_axes, pre...  23.4 us
    all_gather x2, blocking collectives, backward(): lax.all_gather(value.astype(jnp.bfloat16), 'col', axis=0, tiled=True)  20.1 us
  transfers between devices with their start and end apart: 11, of which 11 were waited for; matrix products, arithmetic and copies ran while one was open for 0% of the time, Pallas kernels for 0%

commit v1 on v0

--- a/solution.py
+++ b/solution.py
@@ -11,7 +11,7 @@
 
 def spread(block, axis, source):
     block = jnp.where(lax.axis_index(axis) == source, block, jnp.zeros_like(block))
-    return lax.psum(block, axis)
+    return jnp.sum(lax.all_gather(block, axis), axis=0)
 
 
 def shards(

time: 493 us -> 464 us (0.941)
  waiting for transfers between devices: 365 us -> 319 us
  blocking collectives: 42.9 us -> 54.5 us
    psum x2 -> x0, waiting for transfers between devices: 43.5 us -> none  [spread(): return lax.psum(block, axis)]
    all_gather x0 -> x2, blocking collectives: none -> 11.6 us  [spread(): return jnp.sum(lax.all_gather(block, axis), axis=0)]
  transfers between devices with their start and end apart: 11 -> 9, of which waited for: 11 -> 9; matrix products, arithmetic and copies ran while one was open for 0% -> 0% of each run, Pallas kernels for 0% -> 0%
where the time goes in v1:
time: 464 us
  waiting for transfers between devices  319 us (69%)
  blocking collectives  54.5 us (12%)
  matrix products  43.1 us (9%)
  other arithmetic  16.8 us (4%)
  between operations  15.8 us (3%)
  local copies, waits for them, and re-layouts  13.8 us (3%)
    psum x2, waiting for transfers between devices, forward(): panel_total = lax.psum(accumulated, 'col')  112 us
    reduce_scatter x2, waiting for transfers between devices, backward(): lax.psum_scatter(partial_value, 'col', scatter_dimension=0, tiled=True)  63.1 us
    psum x1, waiting for transfers between devices, shards(): root_share = lax.psum(root_share, ('sub', 'row'))  57.1 us
    psum x2, waiting for transfers between devices, backward(): summed = lax.psum(contribution + own_couple, 'row')  37.3 us
    reduce_scatter x1, waiting for transfers between devices, shards(): lax.psum_scatter(root_term, 'col', scatter_dimension=0, tiled=True)  26.1 us
    reduce_scatter x1, waiting for transfers between devices, shards(): lax.psum_scatter(lax.dot_general(root_inverse, root_half, first_axes, pre...  23.4 us
    all_gather x2, blocking collectives, backward(): lax.all_gather(value.astype(jnp.bfloat16), 'col', axis=0, tiled=True)  20.1 us
    all_gather x1, blocking collectives, shards(): root_rhs = lax.all_gather(root_share, 'col', axis=0, tiled=True)  12.6 us
  transfers between devices with their start and end apart: 9, of which 9 were waited for; matrix products, arithmetic and copies ran while one was open for 0% of the time, Pallas kernels for 0%

profile of v1, /device:TPU:0, one launch (start us, length us, event | category | flops | bytes accessed | tf_op | source)
XLA Modules:
  0.0 463.6 jit_solution(5283436498615279234)
XLA Ops:
  9.2 5.5 %bitcast_multiply_fusion = bf16[2,512,2048]{2,1,0:T(8,128)(2,1)} fusion(bf16[1,2,512,2048]{3,2,1,0:T(8,128)(2,1)} %param.16, f32[2]{0:T(128)S(1)} %compare_convert_fusion, bf16[2048,16,1]{0,1,2:T(8,128)(2,1)S(1)} %reshape.58, s32[2,512]{1,0:T(2,128)S(1)} %and_select_fusion), kind=kOutput, calls=%fused_computation.24 | convolution fusion | flops 73416704 | bytes 8458248 | tf_op jit(solution)/shard_map/in,nqj->qji/dot_general | solution.py:51
  15.4 150.6 %while.39 = (s32[]{:T(128)}, f32[2048,128]{1,0:T(8,128)}, f32[512,128]{0,1:T(8,128)}, bf16[2,512,2048]{2,1,0:T(8,128)(2,1)}, s32[]{:T(128)}, /*index=5*/f32[2048...) while((s32[]{:T(128)}, f32[2048,128]{1,0:T(8,128)}, ...), condition=%wide.region_5.6_spmd.clone, body=%wide.region_0.5_spmd.clone.sunk | while | flops 1880293376 | bytes 25166120 | solution.py:75
  16.5 58.0 %all-reduce.6.cloned.1.call-done = f32[2048,128]{1,0:T(8,128)} async-done(((f32[2048,128]{1,0:T(8,128)}), f32[2048,128]{1,0:T(8,128)}) %all-reduce.6.cloned.1.call-update) | async-done | bytes 1048592 | tf_op jit(solution)/shard_map/while/body/eval_jaxpr/psum | solution.py:59
  74.5 8.0 %conditional.7 = (f32[512,128]{0,1:T(8,128)}) conditional(s32[]{:T(128)} %convert_element_type.121, f32[512,128]{0,1:T(8,128)} %get-tuple-element.647, (f32[2048,128]{1,0:T(8,128)}, f32[2048,128]{1,0:T(8,128)}, f32[512,2048]{1,0:T(8,128)}) %tuple.122), branch_computations={%region_2.2_spmd.clone, %region_3.3_spmd.clone} | conditional | flops 1610874880 | bytes 6553608
  74.5 8.0 %convolution_bitcast_fusion.1 = f32[512,128]{0,1:T(8,128)} fusion(f32[512,2048]{1,0:T(8,128)} %get-tuple-element.427, f32[2048,128]{1,0:T(8,128)} %get-tuple-element.425, f32[2048,128]{1,0:T(8,128)} %get-tuple-element.426), kind=kOutput, calls=%fused_computation.2 | convolution fusion | flops 1610874880 | bytes 6553600 | tf_op jit(solution)/shard_map/while/body/eval_jaxpr/cond/branch_1_fun/dot_general | solution.py:62
  89.1 3.3 convolution_add_fusion.2
  94.8 54.1 %all-reduce.6.cloned.1.call-done = f32[2048,128]{1,0:T(8,128)} async-done(((f32[2048,128]{1,0:T(8,128)}), f32[2048,128]{1,0:T(8,128)}) %all-reduce.6.cloned.1.call-update) | async-done | bytes 1048592 | tf_op jit(solution)/shard_map/while/body/eval_jaxpr/psum | solution.py:59
  149.8 9.5 %all-gather.3 = bf16[1024,128]{0,1:T(8,128)(2,1)} all-gather(bf16[512,128]{0,1:T(8,128)(2,1)S(1)} %convert_select_fusion.2), channel_id=2, replica_groups=mesh['sub'=4,'row'=2,'col'=4] {'row'}, dimensions={0}, use_global_device_ids=true | all-gather | bytes 393216 | tf_op jit(solution)/shard_map/while/body/eval_jaxpr/all_gather | solution.py:14
  162.7 3.3 convolution_add_fusion.2
  171.7 26.1 %reduce-scatter.4.cloned.1.call-done = f32[384,128]{1,0:T(8,128)} async-done(((f32[1536,128]{1,0:T(8,128)}), f32[384,128]{1,0:T(8,128)}) %reduce-scatter.4.cloned.1.call-update) | async-done | bytes 196624 | tf_op jit(solution)/shard_map/reduce_scatter | solution.py:89
  197.9 57.1 %all-reduce.4.cloned.1.call-done = f32[384,128]{1,0:T(8,128)} async-done(((f32[384,128]{1,0:T(8,128)}), f32[384,128]{1,0:T(8,128)}) %all-reduce.4.cloned.1.call-update) | async-done | bytes 196624 | tf_op jit(solution)/shard_map/psum | solution.py:90
  255.0 12.6 %all_gather.36 = f32[1536,128]{1,0:T(8,128)S(1)} all-gather(f32[384,128]{1,0:T(8,128)} %all-reduce.4.cloned.1.call-done), channel_id=1, replica_groups=mesh['sub'=4,'row'=2,'col'=4] {'col'}, dimensions={0}, use_global_device_ids=true | all-gather | bytes 983040 | tf_op jit(solution)/shard_map/all_gather | solution.py:91
  273.8 23.4 %reduce-scatter.6.cloned.1.call-done = f32[384,128]{0,1:T(8,128)} async-done(((f32[1536,128]{0,1:T(8,128)}), f32[384,128]{0,1:T(8,128)}) %reduce-scatter.6.cloned.1.call-update) | async-done | bytes 196624 | tf_op jit(solution)/shard_map/reduce_scatter | solution.py:95
  298.2 10.1 %all_gather.37 = bf16[1536,128]{0,1:T(8,128)(2,1)S(1)} all-gather(bf16[384,128]{0,1:T(8,128)(2,1)S(1)} %convert_element_type.97), channel_id=1, replica_groups=mesh['sub'=4,'row'=2,'col'=4] {'col'}, dimensions={0}, use_global_device_ids=true | all-gather | bytes 491520 | tf_op jit(solution)/shard_map/all_gather | solution.py:107
  312.3 140.1 %while.40 = (s32[]{:T(128)}, f32[512,128]{0,1:T(8,128)}, bf16[2048,128]{0,1:T(8,128)(2,1)}, s32[]{:T(128)}, bf16[2,512,2048]{2,1,0:T(8,128)(2,1)}, /*index=5*/f3...) while((s32[]{:T(128)}, f32[512,128]{0,1:T(8,128)}, ...), condition=%wide.region_14.15_spmd.clone, body=%wide.region_9.14_spmd.clone.sunk | while | flops 1880293376 | bytes 21758288 | solution.py:141
  315.4 18.9 %all-reduce.8.cloned.1.call-done = f32[512,128]{1,0:T(8,128)} async-done(((f32[512,128]{1,0:T(8,128)}), f32[512,128]{1,0:T(8,128)}) %all-reduce.8.cloned.1.call-update) | async-done | bytes 262160 | tf_op jit(solution)/shard_map/while/body/eval_jaxpr/psum | solution.py:121
  335.4 33.8 %reduce-scatter.8.cloned.1.call-done = f32[512,128]{0,1:T(8,128)} async-done(((f32[2048,128]{0,1:T(8,128)}), f32[512,128]{0,1:T(8,128)}) %reduce-scatter.8.cloned.1.call-update) | async-done | bytes 262160 | tf_op jit(solution)/shard_map/while/body/eval_jaxpr/reduce_scatter | solution.py:134
  371.0 10.1 %all_gather.40 = bf16[2048,128]{0,1:T(8,128)(2,1)S(1)} all-gather(bf16[512,128]{0,1:T(8,128)(2,1)S(1)} %get-tuple-element.630), channel_id=1, replica_groups=mesh['sub'=4,'row'=2,'col'=4] {'col'}, dimensions={0}, use_global_device_ids=true | all-gather | bytes 655360 | tf_op jit(solution)/shard_map/while/body/eval_jaxpr/all_gather | solution.py:135
  382.0 3.2 fusion.50
  385.2 18.4 %all-reduce.8.cloned.1.call-done = f32[512,128]{1,0:T(8,128)} async-done(((f32[512,128]{1,0:T(8,128)}), f32[512,128]{1,0:T(8,128)}) %all-reduce.8.cloned.1.call-update) | async-done | bytes 262160 | tf_op jit(solution)/shard_map/while/body/eval_jaxpr/psum | solution.py:121
  403.6 4.7 %conditional.8 = (f32[2048,128]{0,1:T(8,128)S(1)}) conditional(s32[]{:T(128)} %convert_element_type.123, () %tuple.125, (f32[512,128]{1,0:T(8,128)}, f32[512,128]{1,0:T(8,128)}, f32[512,2048]{1,0:T(8,128)}) %tuple.126), branch_computations={%region_11.11_spmd, %region_12.12_spmd} | conditional | flops 1610678272 | bytes 5767176 | solution.py:122
  403.6 4.7 %convolution_bitcast_fusion = f32[2048,128]{0,1:T(8,128)S(1)} fusion(f32[512,2048]{1,0:T(8,128)} %get-tuple-element.405, f32[512,128]{1,0:T(8,128)} %get-tuple-element.403, f32[512,128]{1,0:T(8,128)} %get-tuple-element.404), kind=kOutput, calls=%fused_computation | convolution fusion | flops 1610678272 | bytes 5767168 | tf_op jit(solution)/shard_map/while/body/eval_jaxpr/cond/branch_1_fun/dot_general | solution.py:124
  409.3 29.3 %reduce-scatter.8.cloned.1.call-done = f32[512,128]{0,1:T(8,128)} async-done(((f32[2048,128]{0,1:T(8,128)}), f32[512,128]{0,1:T(8,128)}) %reduce-scatter.8.cloned.1.call-update) | async-done | bytes 262160 | tf_op jit(solution)/shard_map/while/body/eval_jaxpr/reduce_scatter | solution.py:134
  440.5 10.1 %all_gather.40 = bf16[2048,128]{0,1:T(8,128)(2,1)S(1)} all-gather(bf16[512,128]{0,1:T(8,128)(2,1)S(1)} %get-tuple-element.630), channel_id=1, replica_groups=mesh['sub'=4,'row'=2,'col'=4] {'col'}, dimensions={0}, use_global_device_ids=true | all-gather | bytes 655360 | tf_op jit(solution)/shard_map/while/body/eval_jaxpr/all_gather | solution.py:135
  (78 shorter events, 48.3 us)
Async XLA Ops:
  8.0 259.6 %copy-start = (f32[384,1536]{1,0:T(8,128)S(1)}, f32[384,1536]{1,0:T(8,128)}, u32[]{:S(2)}) copy-start(f32[384,1536]{1,0:T(8,128)} %param.21) | copy-start | bytes 7077892
  15.4 152.3 %copy-start.7 = (s32[1,1024]{1,0:T(1,128)S(1)}, s32[1,1024]{1,0:T(1,128)}, u32[]{:S(2)}) copy-start(s32[1,1024]{1,0:T(1,128)} %param.20) | copy-start | bytes 12292
  15.4 59.1 %all-reduce.6.cloned.1.call-start = ((), (), s32[]{:S(2)}) async-start(), calls=%async_computation.6 | async-start | bytes 2097152 | tf_op jit(solution)/shard_map/while/body/eval_jaxpr/psum | solution.py:59
  16.5 72.6 %copy-start.1 = (f32[2048,128]{1,0:T(8,128)S(1)}, f32[2048,128]{1,0:T(8,128)}, u32[]{:S(2)}) copy-start(f32[2048,128]{1,0:T(8,128)} %broadcast_select_fusion.7) | copy-start | bytes 3145732 | tf_op jit(solution)/shard_map/while
  92.5 56.4 %all-reduce.6.cloned.1.call-start = ((), (), s32[]{:S(2)}) async-start(), calls=%async_computation.6 | async-start | bytes 2097152 | tf_op jit(solution)/shard_map/while/body/eval_jaxpr/psum | solution.py:59
  94.7 68.0 %copy-start.1 = (f32[2048,128]{1,0:T(8,128)S(1)}, f32[2048,128]{1,0:T(8,128)}, u32[]{:S(2)}) copy-start(f32[2048,128]{1,0:T(8,128)} %broadcast_select_fusion.7) | copy-start | bytes 3145732 | tf_op jit(solution)/shard_map/while
  166.1 4.6 copy-start.6
  166.1 31.7 %reduce-scatter.4.cloned.1.call-start = ((), (), s32[]{:S(2)}) async-start(), calls=%async_computation.3 | async-start | bytes 983040 | tf_op jit(solution)/shard_map/reduce_scatter | solution.py:89
  170.7 0.9 copy-start.5
  171.6 83.3 %all-reduce.4.cloned.1.call-start = ((), (), s32[]{:S(2)}) async-start(), calls=%async_computation.4 | async-start | bytes 393216 | tf_op jit(solution)/shard_map/psum | solution.py:90
  197.8 75.1 %copy-start.3 = (f32[512,128]{0,1:T(8,128)S(1)}, f32[512,128]{0,1:T(8,128)}, u32[]{:S(2)}) copy-start(f32[512,128]{0,1:T(8,128)} %get-tuple-element.497) | copy-start | bytes 786436
  197.8 99.4 %reduce-scatter.6.cloned.1.call-start = ((), (), s32[]{:S(2)}) async-start(), calls=%async_computation.5 | async-start | bytes 983040 | tf_op jit(solution)/shard_map/reduce_scatter | solution.py:95
  273.8 35.6 %copy-start.4 = (bf16[1,1,512,1024]{3,2,1,0:T(8,128)(2,1)S(1)}, bf16[1,1,512,1024]{3,2,1,0:T(8,128)(2,1)}, u32[]{:S(2)}) copy-start(bf16[1,1,512,1024]{3,2,1,0:T(8,128)(2,1)} %param.19) | copy-start | bytes 3145732
  312.4 22.0 %all-reduce.8.cloned.1.call-start = ((), (), s32[]{:S(2)}) async-start(), calls=%async_computation.7 | async-start | bytes 524288 | tf_op jit(solution)/shard_map/while/body/eval_jaxpr/psum | solution.py:121
  315.4 53.8 %reduce-scatter.8.cloned.1.call-start = ((), (), s32[]{:S(2)}) async-start(), calls=%async_computation.8 | async-start | bytes 1310720 | tf_op jit(solution)/shard_map/while/body/eval_jaxpr/reduce_scatter | solution.py:134
  334.4 1.0 copy-start.2
  382.0 21.6 %all-reduce.8.cloned.1.call-start = ((), (), s32[]{:S(2)}) async-start(), calls=%async_computation.7 | async-start | bytes 524288 | tf_op jit(solution)/shard_map/while/body/eval_jaxpr/psum | solution.py:121
  385.1 53.4 %reduce-scatter.8.cloned.1.call-start = ((), (), s32[]{:S(2)}) async-start(), calls=%async_computation.8 | async-start | bytes 1310720 | tf_op jit(solution)/shard_map/while/body/eval_jaxpr/reduce_scatter | solution.py:134
  408.3 1.0 copy-start.2
Sparse Core Ops, SparseCore 0:
  19.3 55.1 all-reduce.5
  96.3 52.4 all-reduce.5
  316.0 18.2 all-reduce.7
  337.1 32.1 reduce-scatter.7
  385.3 18.1 all-reduce.7
  409.4 29.1 reduce-scatter.7
Sparse Core Ops, SparseCore 1:
  171.7 26.0 reduce-scatter.3
  200.0 54.9 all-reduce.3
  273.0 24.2 reduce-scatter.5
